TPU v7x, 512 devices: a whole 4x8x8 slice. The times are simulated.
512 devices in a mesh: blk: 64 (over z, y_hi, core), split: 8 (over x, y_lo).
Axes of the slice: x: 4, y: 8 (y_hi: 4, y_lo: 2; y = y_hi * 2 + y_lo), z: 8, core: 2. Of those that a mesh axis runs over, the one named last changes fastest.
Arguments:
- user_factors: float32 [131072, 512], P(('blk', 'split')), may hold values from -2 to 2
- item_factors: float32 [8192, 512], P('blk'), may hold values from -2 to 2
- obs_items: int32 [131072, 4, 8], P(('blk', 'split')), may hold values from 0 to 127
- obs_conf: int32 [131072, 4, 8], P(('blk', 'split')), may hold values from 1 to 3
Outputs:
- users_out: float32 [131072, 512], P(('blk', 'split'))
- items_out: float32 [8192, 512], P(('blk', 'split'))
All inputs are finite; a program needn't handle non-finite values.
Results may differ from a plain program's by a relative error of at most 0.0003.
Values sent between devices are 32-bit elements; how exact they have to be, the bound alone decides.
No kernel may reach another device: no remote copies, remote signals or barrier semaphores. Data moves between devices by JAX's collectives and lax.ppermute only.
A program may use at most 64 MiB of HBM per device.

v0:
```python
import jax
import jax.numpy as jnp
from jax import lax
from jax.sharding import PartitionSpec as P

SUBS = 4
LEARN_RATE = 0.0005
CONF_SCALE = 0.5
RIDGE_COEF = 0.01


def passed_along(block, axis, distance):
    devices = range(lax.axis_size(axis))
    route = [((i - distance) % len(devices), i) for i in devices]
    return lax.ppermute(block, axis, route)


def dense_counts(obs_rows, conf_rows, slab_rows):
    columns = lax.broadcasted_iota(jnp.int32, (1, 1, slab_rows), 2)
    hits = jnp.where(
        obs_rows[:, :, None] == columns, conf_rows[:, :, None].astype(jnp.float32), jnp.float32(0.0)
    )
    return jnp.sum(hits, axis=1)


def block_step(user_rows, held, counts):
    scores = lax.dot_general(
        user_rows,
        held,
        (((1,), (1,)), ((), ())),
        precision=lax.Precision.HIGHEST,
        preferred_element_type=jnp.float32,
    )
    target = jnp.where(counts > 0, 1.0, 0.0).astype(jnp.float32)
    weights = 1.0 + CONF_SCALE * counts
    errors = weights * (scores - target)
    grad_user = (
        jnp.dot(errors, held, precision=lax.Precision.HIGHEST, preferred_element_type=jnp.float32)
        + RIDGE_COEF * user_rows
    )
    partial_grad = lax.dot_general(
        errors,
        user_rows,
        (((0,), (0,)), ((), ())),
        precision=lax.Precision.HIGHEST,
        preferred_element_type=jnp.float32,
    )
    return (user_rows - LEARN_RATE * grad_user, partial_grad)


def local(user_factors, item_factors, obs_items, obs_conf):
    slab_rows = item_factors.shape[0]
    share_rows = slab_rows // lax.axis_size("split")
    share_start = lax.axis_index("split") * share_rows
    user_rows = user_factors
    held = item_factors
    for step in range(SUBS):
        counts = dense_counts(obs_items[:, step, :], obs_conf[:, step, :], slab_rows)
        user_rows, partial_grad = block_step(user_rows, held, counts)
        total_grad = lax.psum(partial_grad, "split")
        held = held - LEARN_RATE * (total_grad + RIDGE_COEF * held)
        held = passed_along(held, "blk", -1)
    share_out = lax.dynamic_slice_in_dim(held, share_start, share_rows, 0)
    return (user_rows, share_out)


def solution(mesh):
    in_specs = (
        P(("blk", "split"), None),
        P("blk", None),
        P(("blk", "split"), None, None),
        P(("blk", "split"), None, None),
    )
    out_specs = (P(("blk", "split"), None), P(("blk", "split"), None))
    return jax.shard_map(local, mesh=mesh, in_specs=in_specs, out_specs=out_specs, check_vma=False)
```

profile of v0, /device:TPU:17, one launch (start us, length us, event | category | flops | bytes accessed | tf_op | source)
XLA Modules:
  0.0 404.4 jit_solution(9950264955979071427)
XLA Ops:
  7.2 0.0 copy-start
  7.2 0.0 all-reduce.5.cloned.1.call-start
  7.2 0.8 slice_bitcast_fusion
  8.0 0.1 copy.14
  8.1 0.8 convert_bitcast_fusion
  8.9 0.0 copy-start.1
  8.9 0.1 copy.15
  9.0 1.3 select_reduce_fusion.3
  10.3 0.0 copy-done
  10.3 0.0 copy-done.1
  10.3 0.6 fusion.11
  10.9 1.2 fusion.12
  12.1 0.0 all-reduce.5.cloned.1.call-update
  12.1 0.0 all-reduce.7.cloned.1.call-start
  12.1 0.1 copy.16
  12.3 0.1 copy.17
  12.4 83.0 %all-reduce.5.cloned.1.call-done = f32[128,512]{1,0:T(8,128)} async-done(((f32[128,512]{1,0:T(8,128)}), f32[128,512]{1,0:T(8,128)}) %all-reduce.5.cloned.1.call-update) | async-done | bytes 262160 | tf_op jit(solution)/shard_map/psum | solution.py:60
  95.4 1.0 multiply_subtract_fusion.3
  96.4 7.8 %collective-permute-start = (f32[128,512]{1,0:T(8,128)S(1)}, f32[128,512]{1,0:T(8,128)S(1)}, u32[]{:S(2)}, u32[]{:S(2)}) collective-permute-start(f32[128,512]{1,0:T(8,128)S(1)} %multiply_subtract_fusion.3), channel_id=1, source_target_pairs={{8,0},{16,8},{24,16},{32,24},{40,32},{48,40},{56,48},{64,56},{72,6... | collective-permute-start | bytes 786440 | tf_op jit(solution)/shard_map/ppermute | solution.py:15
  104.3 1.3 select_reduce_fusion.2
  105.5 0.7 fusion.7
  106.2 6.7 %collective-permute-done = f32[128,512]{1,0:T(8,128)S(1)} collective-permute-done((f32[128,512]{1,0:T(8,128)S(1)}, f32[128,512]{1,0:T(8,128)S(1)}, u32[]{:S(2)}, u32[]{:S(2)}) %collective-permute-start) | collective-permute-done | bytes 262176 | tf_op jit(solution)/shard_map/ppermute | solution.py:15
  112.9 0.6 fusion.10
  113.5 1.2 fusion.13
  114.6 0.0 all-reduce.7.cloned.1.call-update
  114.7 0.0 all-reduce.9.cloned.1.call-start
  114.7 0.1 copy.18
  114.9 0.1 copy.19
  115.0 75.2 %all-reduce.7.cloned.1.call-done = f32[128,512]{1,0:T(8,128)} async-done(((f32[128,512]{1,0:T(8,128)}), f32[128,512]{1,0:T(8,128)}) %all-reduce.7.cloned.1.call-update) | async-done | bytes 262160 | tf_op jit(solution)/shard_map/psum | solution.py:60
  190.2 1.0 multiply_subtract_fusion.2
  191.2 7.8 %collective-permute-start.1 = (f32[128,512]{1,0:T(8,128)S(1)}, f32[128,512]{1,0:T(8,128)S(1)}, u32[]{:S(2)}, u32[]{:S(2)}) collective-permute-start(f32[128,512]{1,0:T(8,128)S(1)} %multiply_subtract_fusion.2), channel_id=1, source_target_pairs={{8,0},{16,8},{24,16},{32,24},{40,32},{48,40},{56,48},{64,56},{72,6... | collective-permute-start | bytes 786440 | tf_op jit(solution)/shard_map/ppermute | solution.py:15
  199.0 1.3 select_reduce_fusion.1
  200.3 0.7 fusion.5
  201.0 6.7 %collective-permute-done.1 = f32[128,512]{1,0:T(8,128)S(1)} collective-permute-done((f32[128,512]{1,0:T(8,128)S(1)}, f32[128,512]{1,0:T(8,128)S(1)}, u32[]{:S(2)}, u32[]{:S(2)}) %collective-permute-start.1) | collective-permute-done | bytes 262176 | tf_op jit(solution)/shard_map/ppermute | solution.py:15
  207.7 0.6 fusion.9
  208.3 1.2 fusion.14
  209.4 0.0 all-reduce.9.cloned.1.call-update
  209.5 0.0 all-reduce.11.cloned.1.call-start
  209.5 0.1 copy.20
  209.6 0.1 copy.21
  209.8 75.2 %all-reduce.9.cloned.1.call-done = f32[128,512]{1,0:T(8,128)} async-done(((f32[128,512]{1,0:T(8,128)}), f32[128,512]{1,0:T(8,128)}) %all-reduce.9.cloned.1.call-update) | async-done | bytes 262160 | tf_op jit(solution)/shard_map/psum | solution.py:60
  285.0 1.0 multiply_subtract_fusion.1
  286.0 7.8 %collective-permute-start.2 = (f32[128,512]{1,0:T(8,128)S(1)}, f32[128,512]{1,0:T(8,128)S(1)}, u32[]{:S(2)}, u32[]{:S(2)}) collective-permute-start(f32[128,512]{1,0:T(8,128)S(1)} %multiply_subtract_fusion.1), channel_id=1, source_target_pairs={{8,0},{16,8},{24,16},{32,24},{40,32},{48,40},{56,48},{64,56},{72,6... | collective-permute-start | bytes 786440 | tf_op jit(solution)/shard_map/ppermute | solution.py:15
  293.8 1.3 select_reduce_fusion
  295.1 0.7 fusion.3
  295.7 6.7 %collective-permute-done.2 = f32[128,512]{1,0:T(8,128)S(1)} collective-permute-done((f32[128,512]{1,0:T(8,128)S(1)}, f32[128,512]{1,0:T(8,128)S(1)}, u32[]{:S(2)}, u32[]{:S(2)}) %collective-permute-start.2) | collective-permute-done | bytes 262176 | tf_op jit(solution)/shard_map/ppermute | solution.py:15
  302.5 0.6 fusion.8
  303.0 1.2 fusion.15
  304.2 0.0 all-reduce.11.cloned.1.call-update
  304.2 75.6 %all-reduce.11.cloned.1.call-done = f32[128,512]{1,0:T(8,128)} async-done(((f32[128,512]{1,0:T(8,128)}), f32[128,512]{1,0:T(8,128)}) %all-reduce.11.cloned.1.call-update) | async-done | bytes 262160 | tf_op jit(solution)/shard_map/psum | solution.py:60
  379.8 1.0 multiply_subtract_fusion
  380.8 7.8 %collective-permute-start.3 = (f32[128,512]{1,0:T(8,128)S(1)}, f32[128,512]{1,0:T(8,128)S(1)}, u32[]{:S(2)}, u32[]{:S(2)}) collective-permute-start(f32[128,512]{1,0:T(8,128)S(1)} %multiply_subtract_fusion), channel_id=1, source_target_pairs={{8,0},{16,8},{24,16},{32,24},{40,32},{48,40},{56,48},{64,56},{72,6... | collective-permute-start | bytes 786440 | tf_op jit(solution)/shard_map/ppermute | solution.py:15
  388.6 1.5 fusion.1
  390.1 7.2 %collective-permute-done.3 = f32[128,512]{1,0:T(8,128)S(1)} collective-permute-done((f32[128,512]{1,0:T(8,128)S(1)}, f32[128,512]{1,0:T(8,128)S(1)}, u32[]{:S(2)}, u32[]{:S(2)}) %collective-permute-start.3) | collective-permute-done | bytes 262176 | tf_op jit(solution)/shard_map/ppermute | solution.py:15
  397.3 0.6 constant_dynamic-slice_fusion
Async XLA Ops:
  7.2 3.1 copy-start
  7.2 88.2 %all-reduce.5.cloned.1.call-start = ((), (), s32[]{:S(2)}) async-start(), calls=%async_computation | async-start | bytes 524288 | tf_op jit(solution)/shard_map/psum | solution.py:60
  8.9 1.4 copy-start.1
  12.1 178.1 %all-reduce.7.cloned.1.call-start = ((), (), s32[]{:S(2)}) async-start(), calls=%async_computation.1 | async-start | bytes 524288 | tf_op jit(solution)/shard_map/psum | solution.py:60
  96.4 16.5 %collective-permute-start = (f32[128,512]{1,0:T(8,128)S(1)}, f32[128,512]{1,0:T(8,128)S(1)}, u32[]{:S(2)}, u32[]{:S(2)}) collective-permute-start(f32[128,512]{1,0:T(8,128)S(1)} %multiply_subtract_fusion.3), channel_id=1, source_target_pairs={{8,0},{16,8},{24,16},{32,24},{40,32},{48,40},{56,48},{64,56},{72,6... | collective-permute-start | bytes 786440 | tf_op jit(solution)/shard_map/ppermute | solution.py:15
  114.7 170.3 %all-reduce.9.cloned.1.call-start = ((), (), s32[]{:S(2)}) async-start(), calls=%async_computation.2 | async-start | bytes 524288 | tf_op jit(solution)/shard_map/psum | solution.py:60
  191.2 16.5 %collective-permute-start.1 = (f32[128,512]{1,0:T(8,128)S(1)}, f32[128,512]{1,0:T(8,128)S(1)}, u32[]{:S(2)}, u32[]{:S(2)}) collective-permute-start(f32[128,512]{1,0:T(8,128)S(1)} %multiply_subtract_fusion.2), channel_id=1, source_target_pairs={{8,0},{16,8},{24,16},{32,24},{40,32},{48,40},{56,48},{64,56},{72,6... | collective-permute-start | bytes 786440 | tf_op jit(solution)/shard_map/ppermute | solution.py:15
  209.5 170.3 %all-reduce.11.cloned.1.call-start = ((), (), s32[]{:S(2)}) async-start(), calls=%async_computation.3 | async-start | bytes 524288 | tf_op jit(solution)/shard_map/psum | solution.py:60
  286.0 16.5 %collective-permute-start.2 = (f32[128,512]{1,0:T(8,128)S(1)}, f32[128,512]{1,0:T(8,128)S(1)}, u32[]{:S(2)}, u32[]{:S(2)}) collective-permute-start(f32[128,512]{1,0:T(8,128)S(1)} %multiply_subtract_fusion.1), channel_id=1, source_target_pairs={{8,0},{16,8},{24,16},{32,24},{40,32},{48,40},{56,48},{64,56},{72,6... | collective-permute-start | bytes 786440 | tf_op jit(solution)/shard_map/ppermute | solution.py:15
  380.8 16.5 %collective-permute-start.3 = (f32[128,512]{1,0:T(8,128)S(1)}, f32[128,512]{1,0:T(8,128)S(1)}, u32[]{:S(2)}, u32[]{:S(2)}) collective-permute-start(f32[128,512]{1,0:T(8,128)S(1)} %multiply_subtract_fusion), channel_id=1, source_target_pairs={{8,0},{16,8},{24,16},{32,24},{40,32},{48,40},{56,48},{64,56},{72,6... | collective-permute-start | bytes 786440 | tf_op jit(solution)/shard_map/ppermute | solution.py:15
Sparse Core Ops, SparseCore 0:
  12.2 83.1 all-reduce.4
  114.8 75.3 all-reduce.6
  209.6 75.3 all-reduce.8
  304.3 75.3 all-reduce.10
where the time goes:
time: 405 us; the launch traced here: 404 us
  waiting for transfers between devices  336 us (83%)
  starting transfers between devices  31.5 us (8%)
  between operations  14 us (3%)
  matrix products  10.4 us (3%)
  other arithmetic  9.78 us (2%)
    psum x4, waiting for transfers between devices, local(): total_grad = lax.psum(partial_grad, 'split')  309 us
    ppermute x4, starting transfers between devices, passed_along(): return lax.ppermute(block, axis, route)  31.3 us
    ppermute x4, waiting for transfers between devices, passed_along(): return lax.ppermute(block, axis, route)  27.3 us
  transfers between devices with their start and end apart: 8, of which 8 were waited for; matrix products, arithmetic and copies ran while one was open for 2% of the time, Pallas kernels for 0%

commit v1 on v0

--- a/solution.py
+++ b/solution.py
@@ -57,7 +57,7 @@
     for step in range(SUBS):
         counts = dense_counts(obs_items[:, step, :], obs_conf[:, step, :], slab_rows)
         user_rows, partial_grad = block_step(user_rows, held, counts)
-        total_grad = lax.psum(partial_grad, "split")
+        total_grad = jnp.sum(lax.all_gather(partial_grad, "split"), axis=0)
         held = held - LEARN_RATE * (total_grad + RIDGE_COEF * held)
         held = passed_along(held, "blk", -1)
     share_out = lax.dynamic_slice_in_dim(held, share_start, share_rows, 0)

time: 405 us -> 311 us (0.77)
  the two profiles are of different devices: /device:TPU:17 before, /device:TPU:2 now
where the time goes in v1:
time: 311 us; the launch traced here: 310 us
  waiting for transfers between devices  239 us (77%)
  starting transfers between devices  30.4 us (10%)
  between operations  14 us (5%)
  other arithmetic  13.3 us (4%)
  matrix products  11.5 us (4%)
    all_gather x4, waiting for transfers between devices, local(): total_grad = jnp.sum(lax.all_gather(partial_grad, 'split'), axis=0)  219 us
    ppermute x4, starting transfers between devices, passed_along(): return lax.ppermute(block, axis, route)  30.2 us
    ppermute x4, waiting for transfers between devices, passed_along(): return lax.ppermute(block, axis, route)  19.6 us
    reduce_sum x4, other arithmetic, local(): total_grad = jnp.sum(lax.all_gather(partial_grad, 'split'), axis=0)  7.28 us
  transfers between devices with their start and end apart: 8, of which 8 were waited for; matrix products, arithmetic and copies ran while one was open for 3% of the time, Pallas kernels for 0%

profile of v1, /device:TPU:2, one launch (start us, length us, event | category | flops | bytes accessed | tf_op | source)
XLA Modules:
  0.0 310.4 jit_solution(7609418585606376184)
XLA Ops:
  7.2 0.0 copy-start
  7.2 0.0 all-gather.9.cloned.1.call-start
  7.2 0.8 convert_bitcast_fusion
  8.0 0.1 copy.15
  8.2 0.8 slice_bitcast_fusion
  8.9 0.1 copy.14
  9.0 1.3 select_reduce_fusion.3
  10.3 1.7 fusion.11
  12.0 0.0 copy-done
  12.0 0.0 copy-start.1
  12.0 1.2 fusion.12
  13.2 0.0 all-gather.9.cloned.1.call-update
  13.2 0.0 all-gather.11.cloned.1.call-start
  13.3 0.1 copy.17
  13.4 0.1 copy.16
  13.5 60.2 %all-gather.9.cloned.1.call-done = f32[1024,512]{1,0:T(8,128)} async-done(((f32[128,512]{1,0:T(8,128)}), f32[1024,512]{1,0:T(8,128)}) %all-gather.9.cloned.1.call-update) | async-done | bytes 2097168 | tf_op jit(solution)/shard_map/all_gather | solution.py:60
  73.7 1.8 reduce_sum.74
  75.6 0.0 copy-done.1
  75.6 0.1 multiply_subtract_fusion.3
  75.6 7.5 %collective-permute-start = (f32[128,512]{1,0:T(8,128)S(1)}, f32[128,512]{1,0:T(8,128)S(1)}, u32[]{:S(2)}, u32[]{:S(2)}) collective-permute-start(f32[128,512]{1,0:T(8,128)S(1)} %multiply_subtract_fusion.3), channel_id=1, source_target_pairs={{8,0},{16,8},{24,16},{32,24},{40,32},{48,40},{56,48},{64,56},{72,6... | collective-permute-start | bytes 786440 | tf_op jit(solution)/shard_map/ppermute | solution.py:15
  83.2 1.3 select_reduce_fusion.2
  84.5 0.7 fusion.7
  85.1 4.8 %collective-permute-done = f32[128,512]{1,0:T(8,128)S(1)} collective-permute-done((f32[128,512]{1,0:T(8,128)S(1)}, f32[128,512]{1,0:T(8,128)S(1)}, u32[]{:S(2)}, u32[]{:S(2)}) %collective-permute-start) | collective-permute-done | bytes 262176 | tf_op jit(solution)/shard_map/ppermute | solution.py:15
  89.9 0.6 fusion.10
  90.5 1.2 fusion.13
  91.6 0.0 all-gather.11.cloned.1.call-update
  91.7 0.0 all-gather.13.cloned.1.call-start
  91.7 0.1 copy.19
  91.9 0.1 copy.18
  92.0 52.9 %all-gather.11.cloned.1.call-done = f32[1024,512]{1,0:T(8,128)} async-done(((f32[128,512]{1,0:T(8,128)}), f32[1024,512]{1,0:T(8,128)}) %all-gather.11.cloned.1.call-update) | async-done | bytes 2097168 | tf_op jit(solution)/shard_map/all_gather | solution.py:60
  144.9 1.8 reduce_sum.76
  146.7 0.1 multiply_subtract_fusion.2
  146.7 7.5 %collective-permute-start.1 = (f32[128,512]{1,0:T(8,128)S(1)}, f32[128,512]{1,0:T(8,128)S(1)}, u32[]{:S(2)}, u32[]{:S(2)}) collective-permute-start(f32[128,512]{1,0:T(8,128)S(1)} %multiply_subtract_fusion.2), channel_id=1, source_target_pairs={{8,0},{16,8},{24,16},{32,24},{40,32},{48,40},{56,48},{64,56},{72,6... | collective-permute-start | bytes 786440 | tf_op jit(solution)/shard_map/ppermute | solution.py:15
  154.3 1.3 select_reduce_fusion.1
  155.6 0.7 fusion.5
  156.2 4.8 %collective-permute-done.1 = f32[128,512]{1,0:T(8,128)S(1)} collective-permute-done((f32[128,512]{1,0:T(8,128)S(1)}, f32[128,512]{1,0:T(8,128)S(1)}, u32[]{:S(2)}, u32[]{:S(2)}) %collective-permute-start.1) | collective-permute-done | bytes 262176 | tf_op jit(solution)/shard_map/ppermute | solution.py:15
  161.0 0.6 fusion.9
  161.6 1.2 fusion.14
  162.7 0.0 all-gather.13.cloned.1.call-update
  162.8 0.0 all-gather.15.cloned.1.call-start
  162.8 0.1 copy.21
  163.0 0.1 copy.20
  163.1 52.9 %all-gather.13.cloned.1.call-done = f32[1024,512]{1,0:T(8,128)} async-done(((f32[128,512]{1,0:T(8,128)}), f32[1024,512]{1,0:T(8,128)}) %all-gather.13.cloned.1.call-update) | async-done | bytes 2097168 | tf_op jit(solution)/shard_map/all_gather | solution.py:60
  216.0 1.8 reduce_sum.78
  217.8 0.1 multiply_subtract_fusion.1
  217.8 7.5 %collective-permute-start.2 = (f32[128,512]{1,0:T(8,128)S(1)}, f32[128,512]{1,0:T(8,128)S(1)}, u32[]{:S(2)}, u32[]{:S(2)}) collective-permute-start(f32[128,512]{1,0:T(8,128)S(1)} %multiply_subtract_fusion.1), channel_id=1, source_target_pairs={{8,0},{16,8},{24,16},{32,24},{40,32},{48,40},{56,48},{64,56},{72,6... | collective-permute-start | bytes 786440 | tf_op jit(solution)/shard_map/ppermute | solution.py:15
  225.4 1.3 select_reduce_fusion
  226.7 0.7 fusion.3
  227.3 4.8 %collective-permute-done.2 = f32[128,512]{1,0:T(8,128)S(1)} collective-permute-done((f32[128,512]{1,0:T(8,128)S(1)}, f32[128,512]{1,0:T(8,128)S(1)}, u32[]{:S(2)}, u32[]{:S(2)}) %collective-permute-start.2) | collective-permute-done | bytes 262176 | tf_op jit(solution)/shard_map/ppermute | solution.py:15
  232.1 0.6 fusion.8
  232.7 1.2 fusion.15
  233.9 0.0 all-gather.15.cloned.1.call-update
  233.9 53.2 %all-gather.15.cloned.1.call-done = f32[1024,512]{1,0:T(8,128)} async-done(((f32[128,512]{1,0:T(8,128)}), f32[1024,512]{1,0:T(8,128)}) %all-gather.15.cloned.1.call-update) | async-done | bytes 2097168 | tf_op jit(solution)/shard_map/all_gather | solution.py:60
  287.1 1.8 reduce_sum.79
  288.9 0.1 multiply_subtract_fusion
  288.9 7.5 %collective-permute-start.3 = (f32[128,512]{1,0:T(8,128)S(1)}, f32[128,512]{1,0:T(8,128)S(1)}, u32[]{:S(2)}, u32[]{:S(2)}) collective-permute-start(f32[128,512]{1,0:T(8,128)S(1)} %multiply_subtract_fusion), channel_id=1, source_target_pairs={{8,0},{16,8},{24,16},{32,24},{40,32},{48,40},{56,48},{64,56},{72,6... | collective-permute-start | bytes 786440 | tf_op jit(solution)/shard_map/ppermute | solution.py:15
  296.5 1.5 fusion.1
  298.0 5.2 %collective-permute-done.3 = f32[128,512]{1,0:T(8,128)S(1)} collective-permute-done((f32[128,512]{1,0:T(8,128)S(1)}, f32[128,512]{1,0:T(8,128)S(1)}, u32[]{:S(2)}, u32[]{:S(2)}) %collective-permute-start.3) | collective-permute-done | bytes 262176 | tf_op jit(solution)/shard_map/ppermute | solution.py:15
  303.2 0.6 constant_dynamic-slice_fusion
Async XLA Ops:
  7.2 4.8 %copy-start = (f32[256,512]{1,0:T(8,128)S(1)}, f32[256,512]{1,0:T(8,128)}, u32[]{:S(2)}) copy-start(f32[256,512]{1,0:T(8,128)} %param.4) | copy-start | bytes 1572868
  7.2 66.6 %all-gather.9.cloned.1.call-start = ((), (), s32[]{:S(2)}) async-start(), calls=%async_computation | async-start | bytes 2359296 | tf_op jit(solution)/shard_map/all_gather | solution.py:60
  12.0 63.6 %copy-start.1 = (f32[128,512]{1,0:T(8,128)S(1)}, f32[128,512]{1,0:T(8,128)}, u32[]{:S(2)}) copy-start(f32[128,512]{1,0:T(8,128)} %param.5) | copy-start | bytes 786436
  13.2 131.7 %all-gather.11.cloned.1.call-start = ((), (), s32[]{:S(2)}) async-start(), calls=%async_computation.1 | async-start | bytes 2359296 | tf_op jit(solution)/shard_map/all_gather | solution.py:60
  75.6 14.3 %collective-permute-start = (f32[128,512]{1,0:T(8,128)S(1)}, f32[128,512]{1,0:T(8,128)S(1)}, u32[]{:S(2)}, u32[]{:S(2)}) collective-permute-start(f32[128,512]{1,0:T(8,128)S(1)} %multiply_subtract_fusion.3), channel_id=1, source_target_pairs={{8,0},{16,8},{24,16},{32,24},{40,32},{48,40},{56,48},{64,56},{72,6... | collective-permute-start | bytes 786440 | tf_op jit(solution)/shard_map/ppermute | solution.py:15
  91.7 124.3 %all-gather.13.cloned.1.call-start = ((), (), s32[]{:S(2)}) async-start(), calls=%async_computation.2 | async-start | bytes 2359296 | tf_op jit(solution)/shard_map/all_gather | solution.py:60
  146.7 14.3 %collective-permute-start.1 = (f32[128,512]{1,0:T(8,128)S(1)}, f32[128,512]{1,0:T(8,128)S(1)}, u32[]{:S(2)}, u32[]{:S(2)}) collective-permute-start(f32[128,512]{1,0:T(8,128)S(1)} %multiply_subtract_fusion.2), channel_id=1, source_target_pairs={{8,0},{16,8},{24,16},{32,24},{40,32},{48,40},{56,48},{64,56},{72,6... | collective-permute-start | bytes 786440 | tf_op jit(solution)/shard_map/ppermute | solution.py:15
  162.8 124.3 %all-gather.15.cloned.1.call-start = ((), (), s32[]{:S(2)}) async-start(), calls=%async_computation.3 | async-start | bytes 2359296 | tf_op jit(solution)/shard_map/all_gather | solution.py:60
  217.8 14.3 %collective-permute-start.2 = (f32[128,512]{1,0:T(8,128)S(1)}, f32[128,512]{1,0:T(8,128)S(1)}, u32[]{:S(2)}, u32[]{:S(2)}) collective-permute-start(f32[128,512]{1,0:T(8,128)S(1)} %multiply_subtract_fusion.1), channel_id=1, source_target_pairs={{8,0},{16,8},{24,16},{32,24},{40,32},{48,40},{56,48},{64,56},{72,6... | collective-permute-start | bytes 786440 | tf_op jit(solution)/shard_map/ppermute | solution.py:15
  288.9 14.3 %collective-permute-start.3 = (f32[128,512]{1,0:T(8,128)S(1)}, f32[128,512]{1,0:T(8,128)S(1)}, u32[]{:S(2)}, u32[]{:S(2)}) collective-permute-start(f32[128,512]{1,0:T(8,128)S(1)} %multiply_subtract_fusion), channel_id=1, source_target_pairs={{8,0},{16,8},{24,16},{32,24},{40,32},{48,40},{56,48},{64,56},{72,6... | collective-permute-start | bytes 786440 | tf_op jit(solution)/shard_map/ppermute | solution.py:15
Sparse Core Ops, SparseCore 0:
  13.3 60.3 all-gather.8
  91.8 53.0 all-gather.10
  162.9 53.0 all-gather.12
  234.0 53.0 all-gather.14
